TPU v7x, 256 devices: a whole 4x4x8 slice. The times are simulated.
256 devices in a mesh: phase: 4 (over x), ctx: 64 (over z, y, core).
Axes of the slice: x: 4, y: 4, z: 8, core: 2. Of those that a mesh axis runs over, the one named last changes fastest.
Arguments:
- hidden: bfloat16 [4, 8192, 4096], P('phase', 'ctx'), may hold values from -6 to 6
- queries: bfloat16 [4, 8192, 2048], P('phase', 'ctx'), may hold values from -400 to 400
- key_value_weight: bfloat16 [4, 4096, 1024], P('phase'), may hold values from -0.09375 to 0.09375
- doc_ids: int32 [4, 8192], P('phase'), may hold values from 0 to 7, never falling along the last dimension, each value on 1 to 6144 neighbouring positions
- scored: int32 [4, 8192], P('phase', 'ctx'), may hold values 0 or 1
Outputs:
- passed: bfloat16 [4, 8192, 2048], P('phase', 'ctx')
Inputs may be any that keep to these rules, and one draw needn't show every extreme that they name: doc_ids never fall along a sequence; one document spans exactly 6144 tokens.
All inputs are finite; a program needn't handle non-finite values. No bound on the sum of `scored` on one device may be relied on, other than what follows from the above.
Results may differ from a plain program's by a relative error of at most 0.008.
The roundings to bfloat16 on the way count: a program that leaves them out, or rounds other values in their place, can miss the bound.
Values may be sent and summed in bfloat16 or wider, within the bound.
A program may use at most 128 MiB of HBM per device.

v0:
```python
import math
import jax
import jax.numpy as jnp
from jax import lax
from jax.sharding import PartitionSpec as P

QUERY_HEADS = 16
KEY_VALUE_HEADS = 4
HEAD_SIZE = 128
rope_base = 500000.0


def from_behind(block, axis, distance):
    devices = range(lax.axis_size(axis))
    route = [((i - distance) % len(devices), i) for i in devices]
    return lax.ppermute(block, axis, route)


def apply_rotary(key_heads, token_positions):
    half_dim = key_heads.shape[-1] // 2
    frequency = rope_base ** (-jnp.arange(half_dim, dtype=jnp.float32) * 2.0 / key_heads.shape[-1])
    angles = token_positions.astype(jnp.float32)[:, None] * frequency[None, :]
    cosine_part = jnp.cos(angles)[:, None, :]
    sine_part = jnp.sin(angles)[:, None, :]
    lower_half = key_heads[..., :half_dim]
    upper_half = key_heads[..., half_dim:]
    return jnp.concatenate(
        [
            lower_half * cosine_part - upper_half * sine_part,
            upper_half * cosine_part + lower_half * sine_part,
        ],
        axis=-1,
    )


def per_device(hidden, queries, key_value_weight, doc_ids, scored):
    count_of_rows = hidden.shape[1]
    first_row = lax.axis_index("ctx") * count_of_rows
    token_positions = first_row + jnp.arange(count_of_rows, dtype=jnp.int32)
    wide = hidden[0].astype(jnp.float32)
    normed = (wide * lax.rsqrt(jnp.mean(wide * wide, axis=-1, keepdims=True) + 1e-05)).astype(
        jnp.bfloat16
    )
    projected_rows = jnp.dot(normed, key_value_weight[0], preferred_element_type=jnp.float32)
    key_value_width = KEY_VALUE_HEADS * HEAD_SIZE
    key_matrix = (
        apply_rotary(
            projected_rows[:, :key_value_width].reshape(count_of_rows, KEY_VALUE_HEADS, HEAD_SIZE),
            token_positions,
        )
        .astype(jnp.bfloat16)
        .reshape(count_of_rows, key_value_width)
    )
    value_matrix = projected_rows[:, key_value_width:].astype(jnp.bfloat16)
    query_group_width = QUERY_HEADS // KEY_VALUE_HEADS
    query_head_count = queries[0].reshape(
        count_of_rows, KEY_VALUE_HEADS, query_group_width, HEAD_SIZE
    )
    sequence_docs = doc_ids[0]
    own_docs = lax.dynamic_slice_in_dim(sequence_docs, first_row, count_of_rows, 0)
    score_scale = 1.0 / math.sqrt(HEAD_SIZE)
    stacked = jnp.concatenate([key_matrix, value_matrix], axis=1)
    collected_rows = lax.all_gather(stacked, "ctx", axis=0, tiled=True)
    sequence_length = collected_rows.shape[0]
    every_key_row = collected_rows[:, :key_value_width].reshape(
        sequence_length, KEY_VALUE_HEADS, HEAD_SIZE
    )
    every_value_row = collected_rows[:, key_value_width:].reshape(
        sequence_length, KEY_VALUE_HEADS, HEAD_SIZE
    )
    head_outputs = []
    for key_value_head in range(KEY_VALUE_HEADS):
        key_part = every_key_row[:, key_value_head : key_value_head + 1]
        key_count = key_part.shape[0]
        scores = (
            jnp.einsum(
                "qhgd,khd->hgqk",
                query_head_count[:, key_value_head : key_value_head + 1],
                key_part,
                preferred_element_type=jnp.float32,
            )
            * score_scale
        )
        key_pos = jnp.arange(key_count, dtype=jnp.int32)
        allowed = (key_pos[None, :] <= token_positions[:, None]) & (
            sequence_docs[None, :] == own_docs[:, None]
        )
        scores = jnp.where(allowed[None, None], scores, jnp.float32(-1e30))
        row_max = jnp.max(scores, axis=-1, keepdims=True)
        expo = jnp.exp(scores - row_max)
        total = jnp.sum(expo, axis=-1)
        weights = expo.astype(jnp.bfloat16)
        summed = jnp.einsum(
            "hgqk,khd->hgqd",
            weights,
            every_value_row[:, key_value_head : key_value_head + 1],
            preferred_element_type=jnp.float32,
        )
        head_outputs.append(summed / total[..., None])
    attended = jnp.transpose(jnp.concatenate(head_outputs, axis=0), (2, 0, 1, 3))
    flat = (
        attended.reshape(count_of_rows, QUERY_HEADS * HEAD_SIZE)
        * scored[0].astype(jnp.float32)[:, None]
    )
    outgoing = flat.astype(jnp.bfloat16)[None]
    return from_behind(outgoing, "phase", 1)


def solution(mesh):
    placed = (
        P("phase", "ctx", None),
        P("phase", "ctx", None),
        P("phase", None, None),
        P("phase", None),
        P("phase", "ctx"),
    )
    return jax.shard_map(
        per_device, mesh=mesh, in_specs=placed, out_specs=P("phase", "ctx", None), check_vma=False
    )
```

profile of v0, /device:TPU:1, one launch (start us, length us, event | category | flops | bytes accessed | tf_op | source)
XLA Modules:
  0.0 297.0 jit_solution(15836771491093661803)
XLA Ops:
  6.5 0.0 all-gather.2.cloned.1.call-start
  6.5 1.5 fusion.27
  8.1 0.0 copy-start.1
  8.1 0.0 copy-start.2
  8.1 0.0 copy-start.3
  8.1 5.1 %fusion.20 = f32[128,1024]{1,0:T(8,128)S(1)} fusion(bf16[1,4096,1024]{2,1,0:T(8,128)(2,1)} %param.7, bf16[1,128,4096]{2,1,0:T(8,128)(2,1)} %param.5, f32[128]{0:T(128)S(1)} %add_rsqrt_fusion), kind=kOutput, calls=%fused_computation.24 | convolution fusion | flops 1075314688 | bytes 9961984 | tf_op jit(solution)/shard_map/dot_general | solution.py:44
  13.2 0.1 reshape.293
  13.3 0.3 multiply_cosine_fusion
  13.7 0.3 subtract_convert_fusion
  13.9 0.2 pad_maximum_fusion.2
  14.2 0.7 pad_maximum_fusion.1
  14.9 0.0 all-gather.2.cloned.1.call-update
  14.9 0.0 copy-done.1
  14.9 0.3 copy.20
  15.2 0.0 copy-done.2
  15.2 0.0 copy-done.3
  15.3 3.9 %fusion.26 = pred[128,8192]{0,1:T(8,128)(4,1)S(1)} fusion(s32[128]{0:T(128)S(1)} %dynamic-slice_bitcast_fusion, s32[128]{0:T(128)S(1)} %get-tuple-element.23, s32[8192]{0:T(1024)S(1)} %bitcast.163), kind=kLoop, calls=%fused_computation.31 | loop fusion | flops 3145728 | bytes 1082368 | tf_op jit(solution)/shard_map/and | solution.py:85
  19.2 100.0 %all-gather.2.cloned.1.call-done = bf16[8192,1024]{1,0:T(8,128)(2,1)} async-done(((bf16[128,1024]{1,0:T(8,128)(2,1)}), bf16[8192,1024]{1,0:T(8,128)(2,1)}) %all-gather.2.cloned.1.call-update) | async-done | bytes 16777232 | tf_op jit(solution)/shard_map/all_gather | solution.py:63
  119.2 11.3 %fusion.57 = (bf16[8192,512]{1,0:T(8,128)(2,1)}, bf16[8192,512]{1,0:T(8,128)(2,1)}) fusion(bf16[8192,1024]{1,0:T(8,128)(2,1)} %all-gather.2.cloned.1.call-done), kind=kLoop, calls=%fused_computation.74 | loop fusion | bytes 33554432 | tf_op jit(solution)/shard_map/slice | solution.py:68
  130.5 11.3 %copy.41 = bf16[8192,512]{0,1:T(8,128)(2,1)} copy(bf16[8192,512]{1,0:T(8,128)(2,1)} %get-tuple-element.5) | data formatting | bytes 16777216 | tf_op jit(solution)/shard_map/reshape | solution.py:68
  141.9 12.5 %reshape.294 = bf16[8192,4,128]{2,1,0:T(4,128)(2,1)} reshape(bf16[8192,512]{1,0:T(8,128)(2,1)} %get-tuple-element.6) | data formatting | bytes 16777216 | tf_op jit(solution)/shard_map/reshape | solution.py:65
  154.4 26.4 %fusion.58 = (bf16[8192,1,128]{2,1,0:T(2,128)(2,1)S(1)}, bf16[8192,1,128]{2,1,0:T(2,128)(2,1)S(1)}, bf16[8192,1,128]{2,1,0:T(2,128)(2,1)}, bf16[8192,1,128]{2,1,0:T(2,128)(2,1)S(1)}) fusion(bf16[8192,4,128]{2,1,0:T(4,128)(2,1)} %reshape.294), kind=kLoop, calls=%fused_computation.75 | loop fusion | bytes 16777216 | tf_op jit(solution)/shard_map/slice | solution.py:73
  180.8 7.3 %fusion.62 = (f32[4,128]{1,0:T(4,128)S(1)}, f32[1,4,128,8192]{2,3,1,0:T(8,128)}) fusion(bf16[128,4,4,128]{0,3,2,1:T(8,128)(2,1)S(1)} %bitcast.158, bf16[8192,1,128]{2,1,0:T(2,128)(2,1)S(1)} %get-tuple-element.7, pred[128,8192]{0,1:T(8,128)(4,1)S(1)} %fusion.26), kind=kOutput, calls=%fused_computation.79 | convolution fusion | flops 1086324224 | bytes 22153216 | tf_op jit(solution)/shard_map/qhgd,khd->hgqk/dot_general | solution.py:76
  188.1 7.3 %fusion.60 = (f32[4,128]{1,0:T(4,128)S(1)}, f32[1,4,128,8192]{2,3,1,0:T(8,128)}) fusion(bf16[128,4,4,128]{0,3,2,1:T(8,128)(2,1)S(1)} %bitcast.159, bf16[8192,1,128]{2,1,0:T(2,128)(2,1)S(1)} %get-tuple-element.8, pred[128,8192]{0,1:T(8,128)(4,1)S(1)} %fusion.26), kind=kOutput, calls=%fused_computation.77 | convolution fusion | flops 1086324224 | bytes 22153216 | tf_op jit(solution)/shard_map/qhgd,khd->hgqk/dot_general | solution.py:76
  195.4 8.0 %fusion = f32[4,128]{1,0:T(4,128)S(1)} fusion(f32[1,4,128,8192]{2,3,1,0:T(8,128)} %get-tuple-element.22, f32[4,128]{1,0:T(4,128)S(1)} %get-tuple-element.21), kind=kLoop, calls=%fused_computation.8 | loop fusion | flops 8388096 | bytes 16781312 | tf_op jit(solution)/shard_map/reduce_sum | solution.py:91
  203.4 8.2 %fusion.32 = f32[1,4,128,128]{2,3,1,0:T(8,128)S(1)} fusion(f32[1,4,128,8192]{2,3,1,0:T(8,128)} %get-tuple-element.22, f32[4,128]{1,0:T(4,128)S(1)} %get-tuple-element.21, bf16[8192,4,128]{0,2,1:T(8,128)(2,1)} %bitcast.152, f32[4,128]{1,0:T(4,128)S(1)} %fusion), kind=kOutput, calls=%fused_computation.45 | convolution fusion | flops 1082195968 | bytes 19140608 | tf_op jit(solution)/shard_map/hgqk,khd->hgqd/dot_general | solution.py:93
  211.6 8.0 %fusion.4 = f32[4,128]{1,0:T(4,128)S(1)} fusion(f32[1,4,128,8192]{2,3,1,0:T(8,128)} %get-tuple-element.18, f32[4,128]{1,0:T(4,128)S(1)} %get-tuple-element.17), kind=kLoop, calls=%fused_computation.12 | loop fusion | flops 8388096 | bytes 16781312 | tf_op jit(solution)/shard_map/reduce_sum | solution.py:91
  219.5 0.0 copy-start
  219.5 8.1 %fusion.44 = f32[1,4,128,128]{2,3,1,0:T(8,128)S(1)} fusion(f32[1,4,128,8192]{2,3,1,0:T(8,128)} %get-tuple-element.18, f32[4,128]{1,0:T(4,128)S(1)} %get-tuple-element.17, bf16[8192,4,128]{0,2,1:T(8,128)(2,1)} %bitcast.153, f32[4,128]{1,0:T(4,128)S(1)} %fusion.4), kind=kOutput, calls=%fused_computation.49 | convolution fusion | flops 1082195968 | bytes 19140608 | tf_op jit(solution)/shard_map/hgqk,khd->hgqd/dot_general | solution.py:93
  227.7 0.0 copy-done
  227.7 7.3 %fusion.61 = (f32[4,128]{1,0:T(4,128)S(1)}, f32[1,4,128,8192]{2,3,1,0:T(8,128)}) fusion(bf16[128,4,4,128]{0,3,2,1:T(8,128)(2,1)S(1)} %bitcast.160, bf16[8192,1,128]{2,1,0:T(2,128)(2,1)S(1)} %copy-done, pred[128,8192]{0,1:T(8,128)(4,1)S(1)} %fusion.26), kind=kOutput, calls=%fused_computation.78 | convolution fusion | flops 1086324224 | bytes 22153216 | tf_op jit(solution)/shard_map/qhgd,khd->hgqk/dot_general | solution.py:76
  235.0 8.0 %fusion.2 = f32[4,128]{1,0:T(4,128)S(1)} fusion(f32[1,4,128,8192]{2,3,1,0:T(8,128)} %get-tuple-element.20, f32[4,128]{1,0:T(4,128)S(1)} %get-tuple-element.19), kind=kLoop, calls=%fused_computation.10 | loop fusion | flops 8388096 | bytes 16781312 | tf_op jit(solution)/shard_map/reduce_sum | solution.py:91
  243.0 8.0 %fusion.38 = f32[1,4,128,128]{2,3,1,0:T(8,128)S(1)} fusion(f32[1,4,128,8192]{2,3,1,0:T(8,128)} %get-tuple-element.20, f32[4,128]{1,0:T(4,128)S(1)} %get-tuple-element.19, bf16[8192,4,128]{0,2,1:T(8,128)(2,1)} %bitcast.154, f32[4,128]{1,0:T(4,128)S(1)} %fusion.2), kind=kOutput, calls=%fused_computation.47 | convolution fusion | flops 1082195968 | bytes 19140608 | tf_op jit(solution)/shard_map/hgqk,khd->hgqd/dot_general | solution.py:93
  250.9 7.3 %fusion.59 = (f32[4,128]{1,0:T(4,128)S(1)}, f32[1,4,128,8192]{2,3,1,0:T(8,128)}) fusion(bf16[128,4,4,128]{0,3,2,1:T(8,128)(2,1)S(1)} %bitcast.161, bf16[8192,1,128]{2,1,0:T(2,128)(2,1)S(1)} %get-tuple-element.10, pred[128,8192]{0,1:T(8,128)(4,1)S(1)} %fusion.26), kind=kOutput, calls=%fused_computation.76 | convolution fusion | flops 1086324224 | bytes 22153216 | tf_op jit(solution)/shard_map/qhgd,khd->hgqk/dot_general | solution.py:76
  258.3 8.0 %fusion.6 = f32[4,128]{1,0:T(4,128)S(1)} fusion(f32[1,4,128,8192]{2,3,1,0:T(8,128)} %get-tuple-element.16, f32[4,128]{1,0:T(4,128)S(1)} %get-tuple-element.15), kind=kLoop, calls=%fused_computation.14 | loop fusion | flops 8388096 | bytes 16781312 | tf_op jit(solution)/shard_map/reduce_sum | solution.py:91
  266.2 8.0 %fusion.50 = f32[1,4,128,128]{2,3,1,0:T(8,128)S(1)} fusion(f32[1,4,128,8192]{2,3,1,0:T(8,128)} %get-tuple-element.16, f32[4,128]{1,0:T(4,128)S(1)} %get-tuple-element.15, bf16[8192,4,128]{0,2,1:T(8,128)(2,1)} %bitcast.155, f32[4,128]{1,0:T(4,128)S(1)} %fusion.6), kind=kOutput, calls=%fused_computation.51 | convolution fusion | flops 1082195968 | bytes 19140608 | tf_op jit(solution)/shard_map/hgqk,khd->hgqd/dot_general | solution.py:93
  274.2 0.1 pad_maximum_fusion
  274.3 0.3 copy.36
  274.6 0.1 multiply_convert_fusion
  274.8 1.3 collective-permute-start
  276.0 13.3 %collective-permute-done = bf16[1,128,2048]{2,1,0:T(8,128)(2,1)S(1)} collective-permute-done((bf16[1,128,2048]{2,1,0:T(8,128)(2,1)S(1)}, bf16[1,128,2048]{2,1,0:T(8,128)(2,1)S(1)}, u32[]{:S(2)}, u32[]{:S(2)}) %collective-permute-start) | collective-permute-done | bytes 524320 | tf_op jit(solution)/shard_map/ppermute | solution.py:16
  289.3 0.8 copy.70
  (8 shorter events, 0.1 us)
Async XLA Ops:
  6.5 112.7 %all-gather.2.cloned.1.call-start = ((), (), s32[]{:S(2)}) async-start(), calls=%async_computation | async-start | bytes 17039360 | tf_op jit(solution)/shard_map/all_gather | solution.py:63
  8.1 6.8 %copy-start.1 = (bf16[1,128,2048]{2,1,0:T(8,128)(2,1)S(1)}, bf16[1,128,2048]{2,1,0:T(8,128)(2,1)}, u32[]{:S(2)}) copy-start(bf16[1,128,2048]{2,1,0:T(8,128)(2,1)} %param.6) | copy-start | bytes 1572868
  8.1 7.1 %copy-start.2 = (s32[1,8192]{1,0:T(1,128)S(1)}, s32[1,8192]{1,0:T(1,128)}, u32[]{:S(2)}) copy-start(s32[1,8192]{1,0:T(1,128)} %param.8) | copy-start | bytes 98308
  8.1 7.1 %copy-start.3 = (s32[1,128]{1,0:T(1,128)S(1)}, s32[1,128]{1,0:T(1,128)}, u32[]{:S(2)}) copy-start(s32[1,128]{1,0:T(1,128)} %param.9) | copy-start | bytes 1540
  219.5 8.1 %copy-start = (bf16[8192,1,128]{2,1,0:T(2,128)(2,1)S(1)}, bf16[8192,1,128]{2,1,0:T(2,128)(2,1)}, u32[]{:S(2)}) copy-start(bf16[8192,1,128]{2,1,0:T(2,128)(2,1)} %get-tuple-element.9) | copy-start | bytes 6291460
  274.8 14.6 %collective-permute-start = (bf16[1,128,2048]{2,1,0:T(8,128)(2,1)S(1)}, bf16[1,128,2048]{2,1,0:T(8,128)(2,1)S(1)}, u32[]{:S(2)}, u32[]{:S(2)}) collective-permute-start(bf16[1,128,2048]{2,1,0:T(8,128)(2,1)S(1)} %multiply_convert_fusion), channel_id=1, source_target_pairs={{192,0},{0,64},{64,128},{128,192},{193,1},{1,65},{65,129},{129,193... | collective-permute-start | bytes 1572872 | tf_op jit(solution)/shard_map/ppermute | solution.py:16
Sparse Core Ops, SparseCore 0:
  15.0 104.1 all-gather.1
where the time goes:
time: 298 us; the launch traced here: 297 us
  waiting for transfers between devices  113 us (38%)
  matrix products  66.5 us (22%)
  local copies, waits for them, and re-layouts  63.2 us (21%)
  other arithmetic  39.1 us (13%)
  between operations  13.6 us (5%)
    all_gather x1, waiting for transfers between devices, per_device(): collected_rows = lax.all_gather(stacked, 'ctx', axis=0, tiled=True)  100 us
    dot_general x4, matrix products, per_device(): jnp.einsum('hgqk,khd->hgqd', weights, every_value_row[:, key_value_head:k...  32.2 us
    reduce_sum x4, other arithmetic, per_device(): total = jnp.sum(expo, axis=-1)  31.9 us
    dot_general x4, matrix products, per_device(): jnp.einsum('qhgd,khd->hgqk', query_head_count[:, key_value_head:key_value...  29.2 us
    slice x1, local copies, waits for them, and re-layouts, per_device(): key_part = every_key_row[:, key_value_head:key_value_head + 1]  26.4 us
    ppermute x1, waiting for transfers between devices, from_behind(): return lax.ppermute(block, axis, route)  13.3 us
    reshape x1, local copies, waits for them, and re-layouts, per_device(): collected_rows[:, :key_value_width]  12.5 us
    slice x1, local copies, waits for them, and re-layouts, per_device(): collected_rows[:, key_value_width:]  11.3 us
  transfers between devices with their start and end apart: 2, of which 2 were waited for; matrix products, arithmetic and copies ran while one was open for 1% of the time, Pallas kernels for 0%

commit v1 on v0

--- a/solution.py
+++ b/solution.py
@@ -60,7 +60,9 @@
     own_docs = lax.dynamic_slice_in_dim(sequence_docs, first_row, count_of_rows, 0)
     score_scale = 1.0 / math.sqrt(HEAD_SIZE)
     stacked = jnp.concatenate([key_matrix, value_matrix], axis=1)
-    collected_rows = lax.all_gather(stacked, "ctx", axis=0, tiled=True)
+    collected_rows = jnp.concatenate(
+        lax.all_to_all(jnp.stack([stacked for _ in range(lax.psum(1, "ctx"))]), "ctx", 0, 0), 0
+    )
     sequence_length = collected_rows.shape[0]
     every_key_row = collected_rows[:, :key_value_width].reshape(
         sequence_length, KEY_VALUE_HEADS, HEAD_SIZE

time: 298 us -> 520 us (1.74)
  the two profiles are of different devices: /device:TPU:1 before, /device:TPU:48 now
where the time goes in v1:
time: 520 us; the launch traced here: 519 us
  waiting for transfers between devices  382 us (73%)
  matrix products  65.2 us (13%)
  other arithmetic  38.1 us (7%)
  local copies, waits for them, and re-layouts  20.8 us (4%)
  starting transfers between devices  13.4 us (3%)
    all_to_all x1, waiting for transfers between devices, per_device(): lax.all_to_all(jnp.stack([stacked for _ in range(lax.psum(1, 'ctx'))]), '...  368 us
    dot_general x4, matrix products, per_device(): jnp.einsum('hgqk,khd->hgqd', weights, every_value_row[:, key_value_head:k...  32.1 us
    reduce_sum x4, other arithmetic, per_device(): total = jnp.sum(expo, axis=-1)  31.9 us
    dot_general x4, matrix products, per_device(): jnp.einsum('qhgd,khd->hgqk', query_head_count[:, key_value_head:key_value...  28.1 us
    ppermute x1, waiting for transfers between devices, from_behind(): return lax.ppermute(block, axis, route)  13.5 us
    all_to_all x1, starting transfers between devices, per_device(): lax.all_to_all(jnp.stack([stacked for _ in range(lax.psum(1, 'ctx'))]), '...  11.9 us
  transfers between devices with their start and end apart: 2, of which 2 were waited for; matrix products, arithmetic and copies ran while one was open for 1% of the time, Pallas kernels for 0%

profile of v1, /device:TPU:48, one launch (start us, length us, event | category | flops | bytes accessed | tf_op | source)
XLA Modules:
  0.0 519.4 jit_solution(15517045514077093117)
XLA Ops:
  0.0 1.5 fusion.27
  1.5 5.0 fusion.20
  6.6 0.1 reshape.298
  6.7 0.3 multiply_cosine_fusion
  7.0 0.3 subtract_convert_fusion
  7.3 0.2 pad_maximum_fusion.2
  7.6 0.2 copy.27
  7.8 6.2 %stack.2 = bf16[64,128,1024]{1,2,0:T(8,128)(2,1)} broadcast(bf16[128,1024]{0,1:T(8,128)(2,1)S(1)} %copy.27), dimensions={1,2} | broadcast | bytes 17039360 | tf_op jit(solution)/shard_map/stack | solution.py:64
  14.0 0.0 copy-start
  14.0 0.0 copy-start.1
  14.0 0.0 copy-start.2
  14.0 11.9 %all-to-all-start = ((bf16[64,128,1024]{1,2,0:T(8,128)(2,1)}), bf16[64,128,1024]{1,2,0:T(8,128)(2,1)}, u32[]{:S(2)}, u32[]{:S(2)}) async-start(bf16[64,128,1024]{1,2,0:T(8,128)(2,1)} %stack.2), calls=%async_computation | async-start | bytes 33554432 | tf_op jit(solution)/shard_map/all_to_all | solution.py:64
  25.9 0.0 copy-done
  25.9 0.3 copy.30
  26.2 0.0 copy-done.1
  26.2 0.0 copy-done.2
  26.2 3.7 fusion.26
  29.9 368.1 %all-to-all-done = bf16[64,128,1024]{1,2,0:T(8,128)(2,1)} async-done(((bf16[64,128,1024]{1,2,0:T(8,128)(2,1)}), bf16[64,128,1024]{1,2,0:T(8,128)(2,1)}, u32[]{:S(2)}, u32[]{:S(2)}) %all-to-all-start) | async-done | bytes 16777248 | tf_op jit(solution)/shard_map/all_to_all | solution.py:64
  398.0 8.7 %copy_bitcast_fusion = bf16[8192,1024]{0,1:T(8,128)(2,1)S(1)} fusion(bf16[64,128,1024]{1,2,0:T(8,128)(2,1)} %all-to-all-done), kind=kLoop, calls=%fused_computation | loop fusion | bytes 33554432 | tf_op jit(solution)/shard_map/reshape | solution.py:63
  406.7 4.2 fusion.57
  410.9 7.0 %fusion.61 = (f32[4,128]{1,0:T(4,128)S(1)}, f32[1,4,128,8192]{2,3,1,0:T(8,128)}) fusion(bf16[128,4,4,128]{0,3,2,1:T(8,128)(2,1)S(1)} %bitcast.172, bf16[8192,4,128]{0,2,1:T(8,128)(2,1)S(1)} %bitcast.166, pred[128,8192]{0,1:T(8,128)(4,1)S(1)} %fusion.26), kind=kOutput, calls=%fused_computation.79 | convolution fusion | flops 1086324224 | bytes 20056064 | tf_op jit(solution)/shard_map/qhgd,khd->hgqk/dot_general | solution.py:78
  417.9 7.0 %fusion.60 = (f32[4,128]{1,0:T(4,128)S(1)}, f32[1,4,128,8192]{2,3,1,0:T(8,128)}) fusion(bf16[128,4,4,128]{0,3,2,1:T(8,128)(2,1)S(1)} %bitcast.173, bf16[8192,4,128]{0,2,1:T(8,128)(2,1)S(1)} %bitcast.167, pred[128,8192]{0,1:T(8,128)(4,1)S(1)} %fusion.26), kind=kOutput, calls=%fused_computation.78 | convolution fusion | flops 1086324224 | bytes 20056064 | tf_op jit(solution)/shard_map/qhgd,khd->hgqk/dot_general | solution.py:78
  424.9 7.0 %fusion.59 = (f32[4,128]{1,0:T(4,128)S(1)}, f32[1,4,128,8192]{2,3,1,0:T(8,128)}) fusion(bf16[128,4,4,128]{0,3,2,1:T(8,128)(2,1)S(1)} %bitcast.174, bf16[8192,4,128]{0,2,1:T(8,128)(2,1)S(1)} %bitcast.168, pred[128,8192]{0,1:T(8,128)(4,1)S(1)} %fusion.26), kind=kOutput, calls=%fused_computation.77 | convolution fusion | flops 1086324224 | bytes 20056064 | tf_op jit(solution)/shard_map/qhgd,khd->hgqk/dot_general | solution.py:78
  432.0 7.0 %fusion.58 = (f32[4,128]{1,0:T(4,128)S(1)}, f32[1,4,128,8192]{2,3,1,0:T(8,128)}) fusion(bf16[128,4,4,128]{0,3,2,1:T(8,128)(2,1)S(1)} %bitcast.175, bf16[8192,4,128]{0,2,1:T(8,128)(2,1)S(1)} %bitcast.169, pred[128,8192]{0,1:T(8,128)(4,1)S(1)} %fusion.26), kind=kOutput, calls=%fused_computation.76 | convolution fusion | flops 1086324224 | bytes 20056064 | tf_op jit(solution)/shard_map/qhgd,khd->hgqk/dot_general | solution.py:78
  439.0 7.9 %fusion = f32[4,128]{1,0:T(4,128)S(1)} fusion(f32[1,4,128,8192]{2,3,1,0:T(8,128)} %get-tuple-element.18, f32[4,128]{1,0:T(4,128)S(1)} %get-tuple-element.17), kind=kLoop, calls=%fused_computation.9 | loop fusion | flops 8388096 | bytes 16781312 | tf_op jit(solution)/shard_map/reduce_sum | solution.py:93
  447.0 8.2 %fusion.32 = f32[1,4,128,128]{2,3,1,0:T(8,128)S(1)} fusion(f32[1,4,128,8192]{2,3,1,0:T(8,128)} %get-tuple-element.18, f32[4,128]{1,0:T(4,128)S(1)} %get-tuple-element.17, bf16[8192,4,128]{0,2,1:T(8,128)(2,1)} %bitcast.162, f32[4,128]{1,0:T(4,128)S(1)} %fusion), kind=kOutput, calls=%fused_computation.46 | convolution fusion | flops 1082195968 | bytes 19140608 | tf_op jit(solution)/shard_map/hgqk,khd->hgqd/dot_general | solution.py:95
  455.1 8.0 %fusion.2 = f32[4,128]{1,0:T(4,128)S(1)} fusion(f32[1,4,128,8192]{2,3,1,0:T(8,128)} %get-tuple-element.16, f32[4,128]{1,0:T(4,128)S(1)} %get-tuple-element.15), kind=kLoop, calls=%fused_computation.11 | loop fusion | flops 8388096 | bytes 16781312 | tf_op jit(solution)/shard_map/reduce_sum | solution.py:93
  463.1 8.0 %fusion.38 = f32[1,4,128,128]{2,3,1,0:T(8,128)S(1)} fusion(f32[1,4,128,8192]{2,3,1,0:T(8,128)} %get-tuple-element.16, f32[4,128]{1,0:T(4,128)S(1)} %get-tuple-element.15, bf16[8192,4,128]{0,2,1:T(8,128)(2,1)} %bitcast.163, f32[4,128]{1,0:T(4,128)S(1)} %fusion.2), kind=kOutput, calls=%fused_computation.48 | convolution fusion | flops 1082195968 | bytes 19140608 | tf_op jit(solution)/shard_map/hgqk,khd->hgqd/dot_general | solution.py:95
  471.1 8.0 %fusion.4 = f32[4,128]{1,0:T(4,128)S(1)} fusion(f32[1,4,128,8192]{2,3,1,0:T(8,128)} %get-tuple-element.14, f32[4,128]{1,0:T(4,128)S(1)} %get-tuple-element.13), kind=kLoop, calls=%fused_computation.13 | loop fusion | flops 8388096 | bytes 16781312 | tf_op jit(solution)/shard_map/reduce_sum | solution.py:93
  479.1 8.0 %fusion.44 = f32[1,4,128,128]{2,3,1,0:T(8,128)S(1)} fusion(f32[1,4,128,8192]{2,3,1,0:T(8,128)} %get-tuple-element.14, f32[4,128]{1,0:T(4,128)S(1)} %get-tuple-element.13, bf16[8192,4,128]{0,2,1:T(8,128)(2,1)} %bitcast.164, f32[4,128]{1,0:T(4,128)S(1)} %fusion.4), kind=kOutput, calls=%fused_computation.50 | convolution fusion | flops 1082195968 | bytes 19140608 | tf_op jit(solution)/shard_map/hgqk,khd->hgqd/dot_general | solution.py:95
  487.0 8.0 %fusion.6 = f32[4,128]{1,0:T(4,128)S(1)} fusion(f32[1,4,128,8192]{2,3,1,0:T(8,128)} %get-tuple-element.12, f32[4,128]{1,0:T(4,128)S(1)} %get-tuple-element.11), kind=kLoop, calls=%fused_computation.15 | loop fusion | flops 8388096 | bytes 16781312 | tf_op jit(solution)/shard_map/reduce_sum | solution.py:93
  495.0 8.0 %fusion.50 = f32[1,4,128,128]{2,3,1,0:T(8,128)S(1)} fusion(f32[1,4,128,8192]{2,3,1,0:T(8,128)} %get-tuple-element.12, f32[4,128]{1,0:T(4,128)S(1)} %get-tuple-element.11, bf16[8192,4,128]{0,2,1:T(8,128)(2,1)} %bitcast.165, f32[4,128]{1,0:T(4,128)S(1)} %fusion.6), kind=kOutput, calls=%fused_computation.52 | convolution fusion | flops 1082195968 | bytes 19140608 | tf_op jit(solution)/shard_map/hgqk,khd->hgqd/dot_general | solution.py:95
  503.0 0.1 pad_maximum_fusion
  503.1 0.3 copy.42
  503.4 0.1 multiply_convert_fusion
  503.5 1.6 collective-permute-start
  505.1 13.5 %collective-permute-done = bf16[1,128,2048]{2,1,0:T(8,128)(2,1)S(1)} collective-permute-done((bf16[1,128,2048]{2,1,0:T(8,128)(2,1)S(1)}, bf16[1,128,2048]{2,1,0:T(8,128)(2,1)S(1)}, u32[]{:S(2)}, u32[]{:S(2)}) %collective-permute-start) | collective-permute-done | bytes 524320 | tf_op jit(solution)/shard_map/ppermute | solution.py:16
  518.6 0.8 copy.61
  (9 shorter events, 0.1 us)
Async XLA Ops:
  14.0 11.9 %copy-start = (bf16[1,128,2048]{2,1,0:T(8,128)(2,1)S(1)}, bf16[1,128,2048]{2,1,0:T(8,128)(2,1)}, u32[]{:S(2)}) copy-start(bf16[1,128,2048]{2,1,0:T(8,128)(2,1)} %param.6) | copy-start | bytes 1572868
  14.0 12.2 %copy-start.1 = (s32[1,8192]{1,0:T(1,128)S(1)}, s32[1,8192]{1,0:T(1,128)}, u32[]{:S(2)}) copy-start(s32[1,8192]{1,0:T(1,128)} %param.8) | copy-start | bytes 98308
  14.0 12.2 %copy-start.2 = (s32[1,128]{1,0:T(1,128)S(1)}, s32[1,128]{1,0:T(1,128)}, u32[]{:S(2)}) copy-start(s32[1,128]{1,0:T(1,128)} %param.9) | copy-start | bytes 1540
  14.0 384.0 %all-to-all-start = ((bf16[64,128,1024]{1,2,0:T(8,128)(2,1)}), bf16[64,128,1024]{1,2,0:T(8,128)(2,1)}, u32[]{:S(2)}, u32[]{:S(2)}) async-start(bf16[64,128,1024]{1,2,0:T(8,128)(2,1)} %stack.2), calls=%async_computation | async-start | bytes 33554432 | tf_op jit(solution)/shard_map/all_to_all | solution.py:64
  503.5 15.1 %collective-permute-start = (bf16[1,128,2048]{2,1,0:T(8,128)(2,1)S(1)}, bf16[1,128,2048]{2,1,0:T(8,128)(2,1)S(1)}, u32[]{:S(2)}, u32[]{:S(2)}) collective-permute-start(bf16[1,128,2048]{2,1,0:T(8,128)(2,1)S(1)} %multiply_convert_fusion), channel_id=1, source_target_pairs={{192,0},{0,64},{64,128},{128,192},{193,1},{1,65},{65,129},{129,193... | collective-permute-start | bytes 1572872 | tf_op jit(solution)/shard_map/ppermute | solution.py:16
